TPU v7x, 32 devices: a whole 2x2x4 slice. The times are simulated.
32 devices in a mesh: tok: 4 (over y, x), exp: 8 (over z, core).
Axes of the slice: x: 2, y: 2, z: 4, core: 2. Of those that a mesh axis runs over, the one named last changes fastest.
Arguments:
- captured: bfloat16 [2048, 8, 1024], P(('tok', 'exp')), may hold values from -16 to 16
- expert_ids: int32 [2048, 8], P(('tok', 'exp')), may hold values from 0 to 31, all different within a row; in each aligned block of 32 rows (0 to 31, 32 to 63, ...) at most 16 rows name the same one
Outputs:
- whitening: float32 [32, 1024, 1024], P(('tok', 'exp'))
Inputs may be any that keep to these rules, and one draw needn't show every extreme that they name: `expert_ids`: each row names 8 different experts; every expert is named by some row. In each aligned block of 32 token rows no expert is named more than 16 times, and in some block some expert is named exactly 16 times.
All inputs are finite; a program needn't handle non-finite values.
Results may differ from a plain program's by a relative error of at most 0.0003.
Values may be sent and summed in bfloat16 or wider, within the bound.
A program may use at most 64 MiB of HBM per device.

v0:
```python
import jax
import jax.numpy as jnp
from jax import lax
from jax.experimental import pallas as pl
from jax.experimental.pallas import tpu as pltpu
from jax.sharding import PartitionSpec as P

damping = 0.1
BLK = 128
SUB = 8
WINDOW = 2

NN = (((1,), (0,)), ((), ()))
NT = (((1,), (1,)), ((), ()))
TN = (((0,), (0,)), ((), ()))


def split(a):
    hi = a.astype(jnp.bfloat16)
    lo = (a - hi.astype(jnp.float32)).astype(jnp.bfloat16)
    return hi, lo


def dot3(a, b, dims):
    ah, al = a
    bh, bl = b
    d = lambda x, y: lax.dot_general(x, y, dims, preferred_element_type=jnp.float32)
    return d(ah, bh) + (d(ah, bl) + d(al, bh))


def diag_inverse(s_ref):
    count = BLK // SUB
    sub = lax.broadcasted_iota(jnp.int32, (SUB, BLK), 0)
    lane = lax.broadcasted_iota(jnp.int32, (SUB, BLK), 1)
    spread = lambda x: jnp.broadcast_to(x, (SUB, BLK))
    rows = [s_ref[SUB * r : SUB * (r + 1), :] for r in range(count)]
    for p in range(count):
        c0 = SUB * p
        inside = (lane >= c0) & (lane < c0 + SUB)
        cols = [[spread(rows[r][:, c0 + s : c0 + s + 1]) for s in range(SUB)] for r in range(p, count)]
        rows[p] = jnp.where(inside, jnp.where(lane - c0 == sub, 1.0, 0.0), rows[p])
        for r in range(p + 1, count):
            rows[r] = jnp.where(inside, 0.0, rows[r])
        pivots = jnp.ones((SUB, BLK), jnp.float32)
        tops, mults, heads = [], [], []
        for s in range(SUB):
            top = [spread(cols[0][t][s : s + 1, :]) for t in range(s, SUB)]
            inv = 1.0 / top[0]
            pivots = jnp.where(sub == s, top[0], pivots)
            head = spread(rows[p][s : s + 1, :])
            m = jnp.where(sub > s, cols[0][s] * inv, 0.0)
            for t in range(s + 1, SUB):
                cols[0][t] = cols[0][t] - m * top[t - s]
            rows[p] = rows[p] - m * head
            tops.append(top)
            mults.append(inv)
            heads.append(head)
        for r in range(p + 1, count):
            col = cols[r - p]
            acc = rows[r]
            for s in range(SUB):
                m = col[s] * mults[s]
                for t in range(s + 1, SUB):
                    col[t] = col[t] - m * tops[s][t - s]
                acc = acc - m * heads[s]
            rows[r] = acc
        rows[p] = jnp.where(lane <= c0 + sub, rows[p] * lax.rsqrt(pivots), 0.0)
    return jnp.concatenate(rows, axis=0)


def exchange_kernel(ids_ref, in_ref, o_ref, x_ref, wh, wl, s_ref, t_ref, pick, outbox, inbox, stat_out, stat_in, send_sem, recv_sem, stat_sem):
    n = o_ref.shape[0]
    steps = n // BLK
    _, devices, slots, _ = outbox.shape
    entries = in_ref.shape[0] * in_ref.shape[1]
    exp_size = lax.axis_size("exp")
    me = lax.axis_index("tok") * exp_size + lax.axis_index("exp")

    def place(offset):
        peer = lax.rem(me + offset, devices)
        return peer, (peer // exp_size, lax.rem(peer, exp_size))

    def part_of(c):
        part = in_ref[:, :, c * BLK : (c + 1) * BLK].astype(jnp.float32)
        return part.reshape(entries, BLK)

    barrier = pltpu.get_barrier_semaphore()

    def greet(offset, carry):
        pl.semaphore_signal(barrier, inc=1, device_id=place(offset)[1], device_id_type=pl.DeviceIdType.MESH)
        return carry

    lax.fori_loop(1, devices, greet, 0)

    ids = ids_ref[...]
    onehot = lax.broadcasted_iota(jnp.int32, (devices, entries), 0) == ids
    onehot_f = onehot.astype(jnp.float32)
    onehot_b = onehot_f.astype(jnp.bfloat16)
    earlier = (
        lax.broadcasted_iota(jnp.int32, (entries, entries), 0)
        < lax.broadcasted_iota(jnp.int32, (entries, entries), 1)
    ).astype(jnp.float32).astype(jnp.bfloat16)
    before = lax.dot_general(onehot_b, earlier, NN, preferred_element_type=jnp.float32)
    rank = jnp.sum(before * onehot_f, axis=0, keepdims=True).astype(jnp.int32)
    target = ids * slots + rank
    for i in range(0, devices * slots, BLK):
        row = lax.broadcasted_iota(jnp.int32, (BLK, entries), 0) + i
        pick[i : i + BLK, :] = (row == target).astype(jnp.float32).astype(jnp.bfloat16)

    def build(c):
        part = lax.dot_general(
            pick[...], part_of(c).astype(jnp.bfloat16), NN, preferred_element_type=jnp.float32
        )
        outbox[c] = part.reshape(devices, slots, BLK).astype(jnp.bfloat16)
        inbox[c, me] = outbox[c, me]

    def send(c):
        def one(offset, carry):
            peer, device = place(offset)
            pltpu.make_async_remote_copy(
                src_ref=outbox.at[c, peer],
                dst_ref=inbox.at[c, me],
                send_sem=send_sem.at[c],
                recv_sem=recv_sem.at[c],
                device_id=device,
                device_id_type=pl.DeviceIdType.MESH,
            ).start()
            return carry

        lax.fori_loop(1, devices, one, 0)

    def send_stats(offset, carry):
        peer, device = place(offset)
        pltpu.make_async_remote_copy(
            src_ref=stat_out.at[peer],
            dst_ref=stat_in.at[me],
            send_sem=stat_sem.at[0],
            recv_sem=stat_sem.at[1],
            device_id=device,
            device_id_type=pl.DeviceIdType.MESH,
        ).start()
        return carry

    build(0)
    build(1)
    pl.semaphore_wait(barrier, devices - 1)
    send(0)
    counts = jnp.sum(onehot_f, axis=1, keepdims=True)
    squares = jnp.zeros((devices, BLK), jnp.float32)
    for c in range(steps):
        v = part_of(c)
        hi, lo = split(v * v)
        squares = squares + lax.dot_general(onehot_b, hi, NN, preferred_element_type=jnp.float32)
        squares = squares + lax.dot_general(onehot_b, lo, NN, preferred_element_type=jnp.float32)
    squares = jnp.sum(squares, axis=1, keepdims=True)
    top = lax.broadcasted_iota(jnp.int32, (SUB, BLK), 0) < SUB // 2
    for d in range(devices):
        stat_out[d] = jnp.where(
            top, jnp.broadcast_to(counts[d : d + 1, :], (SUB, BLK)), jnp.broadcast_to(squares[d : d + 1, :], (SUB, BLK))
        )
    stat_in[me] = stat_out[me]

    for c in range(2, min(3, steps)):
        build(c)
    lax.fori_loop(1, devices, send_stats, 0)
    for c in range(1, min(WINDOW, steps)):
        send(c)
    for c in range(3, steps):
        build(c)
    o_ref[...] = jnp.zeros_like(o_ref)
    wh[...] = jnp.zeros_like(wh)
    wl[...] = jnp.zeros_like(wl)

    def settle(ref, sem):
        part = ref.at[pl.ds(0, devices - 1)]
        pltpu.make_async_copy(part, part, sem).wait()

    settle(stat_in, stat_sem.at[1])
    total = jnp.sum(stat_in[...], axis=0)
    inv_count = 1.0 / total[0:1, :]
    shift = damping * (total[SUB // 2 : SUB // 2 + 1, :] * inv_count / n)
    eye = (
        lax.broadcasted_iota(jnp.int32, (BLK, BLK), 0) == lax.broadcasted_iota(jnp.int32, (BLK, BLK), 1)
    ).astype(jnp.float32)

    def step(k, carry):
        base = pl.multiple_of(k * BLK, BLK)
        settle(inbox.at[k], recv_sem.at[k])

        @pl.when(k + WINDOW < steps)
        def _():
            send(k + WINDOW)

        x_ref[:, pl.ds(base, BLK)] = (
            inbox[k].astype(jnp.float32).reshape(devices * slots, BLK).astype(jnp.bfloat16)
        )
        for i in range(steps):

            @pl.when(k == i)
            def _():
                a = i * BLK
                gram = lax.dot_general(
                    x_ref[:, a : a + BLK], x_ref[:, : a + BLK], TN, preferred_element_type=jnp.float32
                )
                s = gram[:, a:] * inv_count + shift * eye
                if i:
                    g_hi, g_lo = split(gram[:, :a] * inv_count[:, 0:1])
                    cuts = [(j, min(j + 2 * BLK, a)) for j in range(0, a, 2 * BLK)]
                    low = jnp.concatenate(
                        [dot3((g_hi[:, :e], g_lo[:, :e]), (wh[j:e, :e], wl[j:e, :e]), NT) for j, e in cuts], axis=1
                    )
                    l_hi, l_lo = split(low)
                    s = s - dot3((l_hi, l_lo), (l_hi, l_lo), NT)
                    for j, e in cuts:
                        t_ref[:, j:e] = dot3((l_hi[:, j:], l_lo[:, j:]), (wh[j:a, j:e], wl[j:a, j:e]), NN)
                s_ref[...] = s

        own = diag_inverse(s_ref)
        at = (pl.ds(base, BLK), pl.ds(base, BLK))
        o_ref[at] = own
        own_hi, own_lo = split(own)
        wh[at] = own_hi
        wl[at] = own_lo
        for i in range(1, steps):

            @pl.when(k == i)
            def _():
                a = i * BLK
                row = -dot3((own_hi, own_lo), split(t_ref[:, :a]), NN)
                o_ref[a : a + BLK, :a] = row
                hi, lo = split(row)
                wh[a : a + BLK, :a] = hi
                wl[a : a + BLK, :a] = lo

        return carry

    lax.fori_loop(0, steps, step, 0)
    settle(stat_out, stat_sem.at[0])

    def drain(c, carry):
        settle(outbox.at[c], send_sem.at[c])
        return carry

    lax.fori_loop(0, steps, drain, 0)


def shards(captured, expert_ids):
    devices = lax.axis_size("tok") * lax.axis_size("exp")
    token_rows, top_count, n = captured.shape
    entries = token_rows * top_count
    slots = 2 * entries // devices
    steps = n // BLK
    vmem = pl.BlockSpec(memory_space=pltpu.VMEM)
    bf16, f32 = jnp.bfloat16, jnp.float32
    box = pltpu.VMEM((steps, devices, slots, BLK), bf16)
    stat = pltpu.VMEM((devices, SUB, BLK), f32)
    out = pl.pallas_call(
        exchange_kernel,
        out_shape=pltpu.VMEM((n, n), f32),
        in_specs=[vmem, vmem],
        out_specs=vmem,
        scratch_shapes=[
            pltpu.VMEM((devices * slots, n), bf16),
            pltpu.VMEM((n, n), bf16),
            pltpu.VMEM((n, n), bf16),
            pltpu.VMEM((BLK, BLK), f32),
            pltpu.VMEM((BLK, n), f32),
            pltpu.VMEM((devices * slots, entries), bf16),
            box,
            box,
            stat,
            stat,
            pltpu.SemaphoreType.DMA((steps,)),
            pltpu.SemaphoreType.DMA((steps,)),
            pltpu.SemaphoreType.DMA((2,)),
        ],
        compiler_params=pltpu.CompilerParams(collective_id=0, has_side_effects=True, vmem_limit_bytes=36 << 20),
        name="exchange_whiten",
    )(expert_ids.reshape(1, entries), captured)
    return out[None]


def solution(mesh):
    placed = (P(("tok", "exp"), None, None), P(("tok", "exp"), None))
    return jax.shard_map(
        shards, mesh=mesh, in_specs=placed, out_specs=P(("tok", "exp"), None, None), check_vma=False
    )
```

profile of v0, /device:TPU:1, one launch (start us, length us, event | category | flops | bytes accessed | tf_op | source)
XLA Modules:
  0.0 71.6 jit_solution(17262762000077159456)
XLA Ops:
  0.0 0.8 %copy.4 = s32[64,8]{1,0:T(8,128)S(1)} copy(s32[64,8]{0,1:T(8,128)} %param.3) | data formatting | bytes 4096 | tf_op args[1]
  0.8 0.1 reshape.3.ids_ref
  0.9 0.0 copy-start
  0.9 1.2 %copy-done = bf16[64,8,1024]{2,1,0:T(8,128)(2,1)S(1)} copy-done((bf16[64,8,1024]{2,1,0:T(8,128)(2,1)S(1)}, bf16[64,8,1024]{2,1,0:T(8,128)(2,1)}, u32[]{:S(2)}) %copy-start) | copy-done | bytes 1048600
  2.1 67.5 %exchange_whiten.1 = f32[1024,1024]{1,0:T(8,128)S(1)} custom-call(s32[1,512]{1,0:T(1,128)S(1)} %reshape.3.ids_ref, bf16[64,8,1024]{2,1,0:T(8,128)(2,1)S(1)} %copy-done), custom_call_target="tpu_custom_call" | custom-call | tf_op jit(solution)/shard_map/exchange_whiten/pallas_call | solution.py:257
  69.6 2.0 %copy.6 = f32[1,1024,1024]{2,1,0:T(8,128)} copy(f32[1,1024,1024]{2,1,0:T(8,128)S(1)} %bitcast.1) | data formatting | bytes 8388608
Async XLA Ops:
  0.9 1.2 %copy-start = (bf16[64,8,1024]{2,1,0:T(8,128)(2,1)S(1)}, bf16[64,8,1024]{2,1,0:T(8,128)(2,1)}, u32[]{:S(2)}) copy-start(bf16[64,8,1024]{2,1,0:T(8,128)(2,1)} %in_ref.1) | copy-start | bytes 3145732
where the time goes:
time: 72.1 us; the launch traced here: 71.6 us
  Pallas kernels  67.5 us (94%)
  local copies, waits for them, and re-layouts  4.1 us (6%)
    pallas_call x1, Pallas kernels, shards(): pl.pallas_call(exchange_kernel, out_shape=pltpu.VMEM((n, n), f32), in_spe...  67.5 us
    unnamed x4, local copies, waits for them, and re-layouts  4 us

commit v1 on v0

--- a/solution.py
+++ b/solution.py
@@ -8,7 +8,7 @@
 damping = 0.1
 BLK = 128
 SUB = 8
-WINDOW = 2
+WINDOW = 3
 
 NN = (((1,), (0,)), ((), ()))
 NT = (((1,), (1,)), ((), ()))
@@ -28,12 +28,12 @@
     return d(ah, bh) + (d(ah, bl) + d(al, bh))
 
 
-def diag_inverse(s_ref):
+def diag_inverse(block):
     count = BLK // SUB
     sub = lax.broadcasted_iota(jnp.int32, (SUB, BLK), 0)
     lane = lax.broadcasted_iota(jnp.int32, (SUB, BLK), 1)
     spread = lambda x: jnp.broadcast_to(x, (SUB, BLK))
-    rows = [s_ref[SUB * r : SUB * (r + 1), :] for r in range(count)]
+    rows = [block[SUB * r : SUB * (r + 1), :] for r in range(count)]
     for p in range(count):
         c0 = SUB * p
         inside = (lane >= c0) & (lane < c0 + SUB)
@@ -68,11 +68,37 @@
     return jnp.concatenate(rows, axis=0)
 
 
-def exchange_kernel(ids_ref, in_ref, o_ref, x_ref, wh, wl, s_ref, t_ref, pick, outbox, inbox, stat_out, stat_in, send_sem, recv_sem, stat_sem):
-    n = o_ref.shape[0]
+def whole_block(x_ref, wh, wl, i, inv_count, shift):
+    a = i * BLK
+    eye = (
+        lax.broadcasted_iota(jnp.int32, (BLK, BLK), 0) == lax.broadcasted_iota(jnp.int32, (BLK, BLK), 1)
+    ).astype(jnp.float32)
+    gram = lax.dot_general(x_ref[:, a : a + BLK], x_ref[:, : a + BLK], TN, preferred_element_type=jnp.float32)
+    s = gram[:, a:] * inv_count + shift * eye
+    if not i:
+        return s, None
+    g_hi, g_lo = split(gram[:, :a] * inv_count[:, 0:1])
+    cuts = [(j, min(j + 2 * BLK, a)) for j in range(0, a, 2 * BLK)]
+    low = jnp.concatenate(
+        [dot3((g_hi[:, :e], g_lo[:, :e]), (wh[j:e, :e], wl[j:e, :e]), NT) for j, e in cuts], axis=1
+    )
+    l_hi, l_lo = split(low)
+    s = s - dot3((l_hi, l_lo), (l_hi, l_lo), NT)
+    t = jnp.concatenate(
+        [dot3((l_hi[:, j:], l_lo[:, j:]), (wh[j:a, j:e], wl[j:a, j:e]), NN) for j, e in cuts], axis=1
+    )
+    return s, t
+
+
+def exchange_kernel(
+    ids_ref, in_hbm, o_ref, wh, wl, x_ref, scale_ref, in_ref, s_ref, t_ref, pick, outbox, inbox, stat_out, stat_in,
+    in_sem, send_sem, recv_sem, stat_sem,
+):
+    n = x_ref.shape[1]
     steps = n // BLK
     _, devices, slots, _ = outbox.shape
-    entries = in_ref.shape[0] * in_ref.shape[1]
+    top_count, token_rows = ids_ref.shape
+    entries = token_rows * top_count
     exp_size = lax.axis_size("exp")
     me = lax.axis_index("tok") * exp_size + lax.axis_index("exp")
 
@@ -90,9 +116,19 @@
         pl.semaphore_signal(barrier, inc=1, device_id=place(offset)[1], device_id_type=pl.DeviceIdType.MESH)
         return carry
 
+    load = pltpu.make_async_copy(in_hbm, in_ref, in_sem)
+    load.start()
     lax.fori_loop(1, devices, greet, 0)
 
-    ids = ids_ref[...]
+    lane = lax.broadcasted_iota(jnp.int32, (token_rows, entries), 1)
+    token = lax.broadcasted_iota(jnp.int32, (token_rows, entries), 0)
+    widen = (lane // top_count == token).astype(jnp.float32).astype(jnp.bfloat16)
+    wide = lax.dot_general(
+        ids_ref[...].astype(jnp.float32).astype(jnp.bfloat16), widen, NN, preferred_element_type=jnp.float32
+    )
+    choice = lax.broadcasted_iota(jnp.int32, (top_count, entries), 1) % top_count
+    own_choice = choice == lax.broadcasted_iota(jnp.int32, (top_count, entries), 0)
+    ids = jnp.sum(jnp.where(own_choice, wide, 0.0), axis=0, keepdims=True).astype(jnp.int32)
     onehot = lax.broadcasted_iota(jnp.int32, (devices, entries), 0) == ids
     onehot_f = onehot.astype(jnp.float32)
     onehot_b = onehot_f.astype(jnp.bfloat16)
@@ -106,6 +142,7 @@
     for i in range(0, devices * slots, BLK):
         row = lax.broadcasted_iota(jnp.int32, (BLK, entries), 0) + i
         pick[i : i + BLK, :] = (row == target).astype(jnp.float32).astype(jnp.bfloat16)
+    load.wait()
 
     def build(c):
         part = lax.dot_general(
@@ -153,11 +190,10 @@
         squares = squares + lax.dot_general(onehot_b, hi, NN, preferred_element_type=jnp.float32)
         squares = squares + lax.dot_general(onehot_b, lo, NN, preferred_element_type=jnp.float32)
     squares = jnp.sum(squares, axis=1, keepdims=True)
-    top = lax.broadcasted_iota(jnp.int32, (SUB, BLK), 0) < SUB // 2
+    first = lax.broadcasted_iota(jnp.int32, (devices, BLK), 1) < BLK // 2
+    stats = jnp.where(first, jnp.broadcast_to(counts, (devices, BLK)), jnp.broadcast_to(squares, (devices, BLK)))
     for d in range(devices):
-        stat_out[d] = jnp.where(
-            top, jnp.broadcast_to(counts[d : d + 1, :], (SUB, BLK)), jnp.broadcast_to(squares[d : d + 1, :], (SUB, BLK))
-        )
+        stat_out[d] = stats[d : d + 1, :]
     stat_in[me] = stat_out[me]
 
     for c in range(2, min(3, steps)):
@@ -176,52 +212,46 @@
         pltpu.make_async_copy(part, part, sem).wait()
 
     settle(stat_in, stat_sem.at[1])
-    total = jnp.sum(stat_in[...], axis=0)
-    inv_count = 1.0 / total[0:1, :]
-    shift = damping * (total[SUB // 2 : SUB // 2 + 1, :] * inv_count / n)
-    eye = (
-        lax.broadcasted_iota(jnp.int32, (BLK, BLK), 0) == lax.broadcasted_iota(jnp.int32, (BLK, BLK), 1)
-    ).astype(jnp.float32)
+    total = stat_in[0]
+    for d in range(1, devices):
+        total = total + stat_in[d]
+    spread = lambda x: jnp.broadcast_to(x, (SUB, BLK))
+    inv_count = 1.0 / spread(total[:, 0:1])
+    shift = damping * (spread(total[:, BLK // 2 : BLK // 2 + 1]) * inv_count / n)
+    scale_ref[0] = inv_count
+    scale_ref[1] = shift
+    inv_count, shift = inv_count[0:1, :], shift[0:1, :]
+
+    def take(k):
+        settle(inbox.at[k], recv_sem.at[k])
+        x_ref[:, pl.ds(pl.multiple_of(k * BLK, BLK), BLK)] = (
+            inbox[k].astype(jnp.float32).reshape(devices * slots, BLK).astype(jnp.bfloat16)
+        )
 
     def step(k, carry):
         base = pl.multiple_of(k * BLK, BLK)
-        settle(inbox.at[k], recv_sem.at[k])
 
         @pl.when(k + WINDOW < steps)
         def _():
             send(k + WINDOW)
 
-        x_ref[:, pl.ds(base, BLK)] = (
-            inbox[k].astype(jnp.float32).reshape(devices * slots, BLK).astype(jnp.bfloat16)
-        )
-        for i in range(steps):
+        take(k)
+        for i in range(steps - 1):
 
             @pl.when(k == i)
             def _():
-                a = i * BLK
-                gram = lax.dot_general(
-                    x_ref[:, a : a + BLK], x_ref[:, : a + BLK], TN, preferred_element_type=jnp.float32
-                )
-                s = gram[:, a:] * inv_count + shift * eye
+                s, t = whole_block(x_ref, wh, wl, i, inv_count, shift)
+                s_ref[...] = s
                 if i:
-                    g_hi, g_lo = split(gram[:, :a] * inv_count[:, 0:1])
-                    cuts = [(j, min(j + 2 * BLK, a)) for j in range(0, a, 2 * BLK)]
-                    low = jnp.concatenate(
-                        [dot3((g_hi[:, :e], g_lo[:, :e]), (wh[j:e, :e], wl[j:e, :e]), NT) for j, e in cuts], axis=1
-                    )
-                    l_hi, l_lo = split(low)
-                    s = s - dot3((l_hi, l_lo), (l_hi, l_lo), NT)
-                    for j, e in cuts:
-                        t_ref[:, j:e] = dot3((l_hi[:, j:], l_lo[:, j:]), (wh[j:a, j:e], wl[j:a, j:e]), NN)
-                s_ref[...] = s
-
-        own = diag_inverse(s_ref)
+                    t_ref[:, : i * BLK] = t
+
+        own = diag_inverse(s_ref[...])
         at = (pl.ds(base, BLK), pl.ds(base, BLK))
         o_ref[at] = own
         own_hi, own_lo = split(own)
         wh[at] = own_hi
         wl[at] = own_lo
-        for i in range(1, steps):
+        for i in range(1, steps - 1):
 
             @pl.when(k == i)
             def _():
@@ -234,7 +264,7 @@
 
         return carry
 
-    lax.fori_loop(0, steps, step, 0)
+    lax.fori_loop(0, steps - 1, step, 0)
     settle(stat_out, stat_sem.at[0])
 
     def drain(c, carry):
@@ -242,6 +272,22 @@
         return carry
 
     lax.fori_loop(0, steps, drain, 0)
+    take(steps - 1)
+
+
+def last_kernel(o_ref, wh, wl, x_ref, scale_ref, out_ref, last, sems):
+    n = x_ref.shape[1]
+    done = n - BLK
+    early = pltpu.make_async_copy(o_ref, out_ref.at[pl.ds(0, done)], sems.at[0])
+    early.start()
+    s, t = whole_block(x_ref, wh, wl, n // BLK - 1, scale_ref[0, 0:1, :], scale_ref[1, 0:1, :])
+    own = diag_inverse(s)
+    last[:, done:] = own
+    last[:, :done] = -dot3(split(own), split(t), NN)
+    late = pltpu.make_async_copy(last, out_ref.at[pl.ds(done, BLK)], sems.at[1])
+    late.start()
+    early.wait()
+    late.wait()
 
 
 def shards(captured, expert_ids):
@@ -250,19 +296,25 @@
     entries = token_rows * top_count
     slots = 2 * entries // devices
     steps = n // BLK
+    done = n - BLK
     vmem = pl.BlockSpec(memory_space=pltpu.VMEM)
+    hbm = pl.BlockSpec(memory_space=pltpu.HBM)
     bf16, f32 = jnp.bfloat16, jnp.float32
     box = pltpu.VMEM((steps, devices, slots, BLK), bf16)
-    stat = pltpu.VMEM((devices, SUB, BLK), f32)
-    out = pl.pallas_call(
+    stat = pltpu.VMEM((devices, 1, BLK), f32)
+    parts = pl.pallas_call(
         exchange_kernel,
-        out_shape=pltpu.VMEM((n, n), f32),
-        in_specs=[vmem, vmem],
-        out_specs=vmem,
+        out_shape=[
+            pltpu.VMEM((done, n), f32),
+            pltpu.VMEM((done, done), bf16),
+            pltpu.VMEM((done, done), bf16),
+            pltpu.VMEM((devices * slots, n), bf16),
+            pltpu.VMEM((2, SUB, BLK), f32),
+        ],
+        in_specs=[vmem, hbm],
+        out_specs=[vmem] * 5,
         scratch_shapes=[
-            pltpu.VMEM((devices * slots, n), bf16),
-            pltpu.VMEM((n, n), bf16),
-            pltpu.VMEM((n, n), bf16),
+            pltpu.VMEM((token_rows, top_count, n), bf16),
             pltpu.VMEM((BLK, BLK), f32),
             pltpu.VMEM((BLK, n), f32),
             pltpu.VMEM((devices * slots, entries), bf16),
@@ -270,13 +322,23 @@
             box,
             stat,
             stat,
+            pltpu.SemaphoreType.DMA,
             pltpu.SemaphoreType.DMA((steps,)),
             pltpu.SemaphoreType.DMA((steps,)),
             pltpu.SemaphoreType.DMA((2,)),
         ],
-        compiler_params=pltpu.CompilerParams(collective_id=0, has_side_effects=True, vmem_limit_bytes=36 << 20),
+        compiler_params=pltpu.CompilerParams(collective_id=0, has_side_effects=True, vmem_limit_bytes=50 << 20),
         name="exchange_whiten",
-    )(expert_ids.reshape(1, entries), captured)
+    )(expert_ids.T, captured)
+    out = pl.pallas_call(
+        last_kernel,
+        out_shape=jax.ShapeDtypeStruct((n, n), f32),
+        in_specs=[vmem] * 5,
+        out_specs=pl.BlockSpec(memory_space=pl.ANY),
+        scratch_shapes=[pltpu.VMEM((BLK, n), f32), pltpu.SemaphoreType.DMA((2,))],
+        compiler_params=pltpu.CompilerParams(vmem_limit_bytes=36 << 20),
+        name="whiten_last",
+    )(*parts)
     return out[None]
 
 

time: 72.1 us -> 69.5 us (0.964)
  local copies, waits for them, and re-layouts: 4.1 us -> 0 us
  Pallas kernels: 67.5 us -> 69.1 us
    unnamed x4 -> x0, local copies, waits for them, and re-layouts: 4 us -> none
    pallas_call x1 -> x2, Pallas kernels: 67.5 us -> 69.1 us  [the longest x1 61.6 us: shards(): pl.pallas_call(exchange_kernel, out_shape=[pltpu.VMEM((done, n), f32), pl...]
where the time goes in v1:
time: 69.5 us; the launch traced here: 69.3 us
  Pallas kernels  69.1 us (99%)
    pallas_call x1, Pallas kernels, shards(): pl.pallas_call(exchange_kernel, out_shape=[pltpu.VMEM((done, n), f32), pl...  61.6 us
    pallas_call x1, Pallas kernels, shards(): pl.pallas_call(last_kernel, out_shape=jax.ShapeDtypeStruct((n, n), f32),...  7.53 us

profile of v1, /device:TPU:1, one launch (start us, length us, event | category | flops | bytes accessed | tf_op | source)
XLA Modules:
  0.0 69.3 jit_solution(5762049399605317094)
XLA Ops:
  0.0 61.6 %exchange_whiten.1 = (f32[896,1024]{1,0:T(8,128)S(1)}, bf16[896,896]{1,0:T(8,128)(2,1)S(1)}, bf16[896,896]{1,0:T(8,128)(2,1)S(1)}, bf16[1024,1024]{1,0:T(8,128)(2,1)S(1)}, f32[2,8,128]{2,1,0:T(8,128)S(1)}) custom-call(s32[8,64]{1,0:T(8,128)} %bitcast.2, bf16[64,8,1024]{2,1,0:T(8,128)(2,1)} %in_hbm.1), custom_call_target="tpu_custom_call" | custom-call | tf_op jit(solution)/shard_map/exchange_whiten/pallas_call | solution.py:305
  61.6 7.5 %whiten_last.1 = f32[1024,1024]{1,0:T(8,128)} custom-call(f32[896,1024]{1,0:T(8,128)S(1)} %get-tuple-element.10.o_ref, bf16[896,896]{1,0:T(8,128)(2,1)S(1)} %get-tuple-element.11.wh, bf16[896,896]{1,0:T(8,128)(2,1)S(1)} %get-tuple-element.12.wl, bf16[1024,1024]{1,0:T(8,128)(2,1)S(1)} %get-tuple-element.13.x_ref, f32[2,8,128]{2,1,0:T(8,128)S(1)} %get-tuple-element.14.scale_ref), custom_call_target="tpu_custom_call" | custom-call | tf_op jit(solution)/shard_map/whiten_last/pallas_call | solution.py:333

commit v2 on v1

--- a/solution.py
+++ b/solution.py
@@ -8,6 +8,7 @@
 damping = 0.1
 BLK = 128
 SUB = 8
+PAN = 32
 WINDOW = 3
 
 NN = (((1,), (0,)), ((), ()))
@@ -28,44 +29,85 @@
     return d(ah, bh) + (d(ah, bl) + d(al, bh))
 
 
-def diag_inverse(block):
-    count = BLK // SUB
-    sub = lax.broadcasted_iota(jnp.int32, (SUB, BLK), 0)
-    lane = lax.broadcasted_iota(jnp.int32, (SUB, BLK), 1)
-    spread = lambda x: jnp.broadcast_to(x, (SUB, BLK))
-    rows = [block[SUB * r : SUB * (r + 1), :] for r in range(count)]
-    for p in range(count):
-        c0 = SUB * p
-        inside = (lane >= c0) & (lane < c0 + SUB)
-        cols = [[spread(rows[r][:, c0 + s : c0 + s + 1]) for s in range(SUB)] for r in range(p, count)]
-        rows[p] = jnp.where(inside, jnp.where(lane - c0 == sub, 1.0, 0.0), rows[p])
-        for r in range(p + 1, count):
-            rows[r] = jnp.where(inside, 0.0, rows[r])
-        pivots = jnp.ones((SUB, BLK), jnp.float32)
-        tops, mults, heads = [], [], []
-        for s in range(SUB):
-            top = [spread(cols[0][t][s : s + 1, :]) for t in range(s, SUB)]
-            inv = 1.0 / top[0]
-            pivots = jnp.where(sub == s, top[0], pivots)
-            head = spread(rows[p][s : s + 1, :])
-            m = jnp.where(sub > s, cols[0][s] * inv, 0.0)
-            for t in range(s + 1, SUB):
-                cols[0][t] = cols[0][t] - m * top[t - s]
-            rows[p] = rows[p] - m * head
-            tops.append(top)
-            mults.append(inv)
-            heads.append(head)
-        for r in range(p + 1, count):
-            col = cols[r - p]
-            acc = rows[r]
+def diag_inverse(full):
+    n = full.shape[0]
+    size = min(PAN, n)
+    count = size // SUB
+    sub = lax.broadcasted_iota(jnp.int32, (SUB, n), 0)
+    lane = lax.broadcasted_iota(jnp.int32, (SUB, n), 1)
+    zero = (sub * 0).astype(jnp.float32)
+    spread = lambda x: jnp.broadcast_to(x, (SUB, n))
+    columns = lambda v, c: [spread(v[:, c + t : c + t + 1]) + zero for t in range(SUB)]
+    out = []
+    for b0 in range(0, n, size):
+        rows = [full[SUB * r : SUB * (r + 1), :] for r in range(count)]
+        own = columns(rows[0], b0)
+        side = columns(rows[1], b0)
+        after = columns(rows[1], b0 + SUB)
+        for p in range(count):
+            c0 = b0 + SUB * p
+            more = p + 1 < count
+            inside = (lane >= c0) & (lane < c0 + SUB)
+            row = jnp.where(inside, jnp.where(lane - c0 == sub, 1.0, 0.0), rows[p])
+            below = jnp.where(inside, 0.0, rows[p + 1]) if more else None
+            tops, invs, heads = [], [], []
+            pivots = None
             for s in range(SUB):
-                m = col[s] * mults[s]
-                for t in range(s + 1, SUB):
-                    col[t] = col[t] - m * tops[s][t - s]
-                acc = acc - m * heads[s]
-            rows[r] = acc
-        rows[p] = jnp.where(lane <= c0 + sub, rows[p] * lax.rsqrt(pivots), 0.0)
-    return jnp.concatenate(rows, axis=0)
+                top = {t: spread(own[s][t : t + 1, :]) for t in range(s, SUB)}
+                inv = 1.0 / top[s]
+                pivots = jnp.where(sub >= s, top[s], pivots) if s else top[s]
+                head = spread(row[s : s + 1, :])
+                if s < SUB - 1:
+                    m = jnp.where(sub > s, own[s] * inv, 0.0)
+                    for t in range(s + 1, SUB):
+                        own[t] = own[t] - m * top[t]
+                    row = row - m * head
+                if more:
+                    x = side[s]
+                    m = x * inv
+                    for t in range(s + 1, SUB):
+                        side[t] = side[t] - m * top[t]
+                    below = below - m * head
+                    for t in range(SUB):
+                        after[t] = after[t] - m * spread(x[t : t + 1, :])
+                tops.append(top)
+                invs.append(inv)
+                heads.append(head)
+            rows[p] = row * lax.rsqrt(pivots)
+            if more:
+                rows[p + 1] = below
+            own = after
+            if p + 2 < count:
+                solved = [None] * SUB
+                for t in range(SUB - 1, -1, -1):
+                    v = heads[t]
+                    for k in range(SUB - 1, t, -1):
+                        v = v - tops[t][k] * solved[k]
+                    solved[t] = v * invs[t]
+                for r in range(p + 2, count):
+                    acc = jnp.where(inside, 0.0, rows[r])
+                    for col, v in zip(columns(rows[r], c0), solved):
+                        acc = acc - col * v
+                    rows[r] = acc
+                side = columns(rows[p + 2], c0 + SUB)
+                after = columns(rows[p + 2], c0 + 2 * SUB)
+        lower = [jnp.where(lane <= b0 + SUB * p + sub, rows[p], 0.0) for p in range(count)]
+        out += lower
+        if b0 + size < n:
+            both = jnp.concatenate(
+                [jnp.where(lane >= b0 + size, rows[p], lower[p]) for p in range(count)], axis=0
+            )
+            hi, lo = split(both)
+            update = lax.dot_general(
+                jnp.concatenate([hi, hi, lo], axis=0),
+                jnp.concatenate([hi, lo, hi], axis=0),
+                TN,
+                preferred_element_type=jnp.float32,
+            )
+            rest = full[size:, :]
+            spot = lax.broadcasted_iota(jnp.int32, rest.shape, 1)
+            full = jnp.where((spot >= b0) & (spot < b0 + size), 0.0, rest) - update[b0 + size :, :]
+    return jnp.concatenate(out, axis=0)
 
 
 def whole_block(x_ref, wh, wl, i, inv_count, shift):

time: 69.5 us -> 62.3 us (0.90)
  Pallas kernels: 69.1 us -> 62 us
    pallas_call x1, Pallas kernels: 61.6 us -> 56.7 us  [shards(): pl.pallas_call(exchange_kernel, out_shape=[pltpu.VMEM((done, n), f32), pl...]
    pallas_call x1, Pallas kernels: 7.53 us -> 5.26 us  [shards(): pl.pallas_call(last_kernel, out_shape=jax.ShapeDtypeStruct((n, n), f32),...]
where the time goes in v2:
time: 62.3 us; the launch traced here: 62.1 us
  Pallas kernels  62 us (100%)
    pallas_call x1, Pallas kernels, shards(): pl.pallas_call(exchange_kernel, out_shape=[pltpu.VMEM((done, n), f32), pl...  56.7 us
    pallas_call x1, Pallas kernels, shards(): pl.pallas_call(last_kernel, out_shape=jax.ShapeDtypeStruct((n, n), f32),...  5.26 us

profile of v2, /device:TPU:1, one launch (start us, length us, event | category | flops | bytes accessed | tf_op | source)
XLA Modules:
  0.0 62.1 jit_solution(10100995738429504960)
XLA Ops:
  0.0 56.7 %exchange_whiten.1 = (f32[896,1024]{1,0:T(8,128)S(1)}, bf16[896,896]{1,0:T(8,128)(2,1)S(1)}, bf16[896,896]{1,0:T(8,128)(2,1)S(1)}, bf16[1024,1024]{1,0:T(8,128)(2,1)S(1)}, f32[2,8,128]{2,1,0:T(8,128)S(1)}) custom-call(s32[8,64]{1,0:T(8,128)} %bitcast.2, bf16[64,8,1024]{2,1,0:T(8,128)(2,1)} %in_hbm.1), custom_call_target="tpu_custom_call" | custom-call | tf_op jit(solution)/shard_map/exchange_whiten/pallas_call | solution.py:347
  56.7 5.3 %whiten_last.1 = f32[1024,1024]{1,0:T(8,128)} custom-call(f32[896,1024]{1,0:T(8,128)S(1)} %get-tuple-element.10.o_ref, bf16[896,896]{1,0:T(8,128)(2,1)S(1)} %get-tuple-element.11.wh, bf16[896,896]{1,0:T(8,128)(2,1)S(1)} %get-tuple-element.12.wl, bf16[1024,1024]{1,0:T(8,128)(2,1)S(1)} %get-tuple-element.13.x_ref, f32[2,8,128]{2,1,0:T(8,128)S(1)} %get-tuple-element.14.scale_ref), custom_call_target="tpu_custom_call" | custom-call | tf_op jit(solution)/shard_map/whiten_last/pallas_call | solution.py:375

commit v3 on v2

--- a/solution.py
+++ b/solution.py
@@ -9,7 +9,7 @@
 BLK = 128
 SUB = 8
 PAN = 32
-WINDOW = 3
+WINDOW = 2
 
 NN = (((1,), (0,)), ((), ()))
 NT = (((1,), (1,)), ((), ()))
@@ -160,7 +160,20 @@
 
     load = pltpu.make_async_copy(in_hbm, in_ref, in_sem)
     load.start()
-    lax.fori_loop(1, devices, greet, 0)
+    def far_first(step, carry):
+        exp, tok = lax.axis_index("exp"), lax.axis_index("tok")
+        toks = devices // exp_size
+        j = step // toks
+        peer_exp = lax.select(exp >= exp_size // 2, j, exp_size - 1 - j)
+        peer_tok = lax.rem(toks - 1 - tok + lax.rem(step, toks), toks)
+
+        @pl.when((peer_exp != exp) | (peer_tok != tok))
+        def _():
+            pl.semaphore_signal(barrier, inc=1, device_id=(peer_tok, peer_exp), device_id_type=pl.DeviceIdType.MESH)
+
+        return carry
+
+    lax.fori_loop(0, devices, far_first, 0)
 
     lane = lax.broadcasted_iota(jnp.int32, (token_rows, entries), 1)
     token = lax.broadcasted_iota(jnp.int32, (token_rows, entries), 0)

time: 62.3 us -> 60.6 us (0.973); the launches traced: 62.1 us -> 59.6 us
  Pallas kernels: 62 us -> 59.4 us
    pallas_call x1, Pallas kernels: 56.7 us -> 54.2 us  [shards(): pl.pallas_call(exchange_kernel, out_shape=[pltpu.VMEM((done, n), f32), pl...]
where the time goes in v3:
time: 60.6 us; the launch traced here: 59.6 us
  Pallas kernels  59.4 us (98%)
    pallas_call x1, Pallas kernels, shards(): pl.pallas_call(exchange_kernel, out_shape=[pltpu.VMEM((done, n), f32), pl...  54.2 us
    pallas_call x1, Pallas kernels, shards(): pl.pallas_call(last_kernel, out_shape=jax.ShapeDtypeStruct((n, n), f32),...  5.27 us

profile of v3, /device:TPU:1, one launch (start us, length us, event | category | flops | bytes accessed | tf_op | source)
XLA Modules:
  0.0 59.6 jit_solution(10497762062301417031)
XLA Ops:
  0.0 54.2 %exchange_whiten.1 = (f32[896,1024]{1,0:T(8,128)S(1)}, bf16[896,896]{1,0:T(8,128)(2,1)S(1)}, bf16[896,896]{1,0:T(8,128)(2,1)S(1)}, bf16[1024,1024]{1,0:T(8,128)(2,1)S(1)}, f32[2,8,128]{2,1,0:T(8,128)S(1)}) custom-call(s32[8,64]{1,0:T(8,128)} %bitcast.2, bf16[64,8,1024]{2,1,0:T(8,128)(2,1)} %in_hbm.1), custom_call_target="tpu_custom_call" | custom-call | tf_op jit(solution)/shard_map/exchange_whiten/pallas_call | solution.py:360
  54.2 5.3 %whiten_last.1 = f32[1024,1024]{1,0:T(8,128)} custom-call(f32[896,1024]{1,0:T(8,128)S(1)} %get-tuple-element.10.o_ref, bf16[896,896]{1,0:T(8,128)(2,1)S(1)} %get-tuple-element.11.wh, bf16[896,896]{1,0:T(8,128)(2,1)S(1)} %get-tuple-element.12.wl, bf16[1024,1024]{1,0:T(8,128)(2,1)S(1)} %get-tuple-element.13.x_ref, f32[2,8,128]{2,1,0:T(8,128)S(1)} %get-tuple-element.14.scale_ref), custom_call_target="tpu_custom_call" | custom-call | tf_op jit(solution)/shard_map/whiten_last/pallas_call | solution.py:388

commit v4 on v3

--- a/solution.py
+++ b/solution.py
@@ -26,7 +26,9 @@
     ah, al = a
     bh, bl = b
     d = lambda x, y: lax.dot_general(x, y, dims, preferred_element_type=jnp.float32)
-    return d(ah, bh) + (d(ah, bl) + d(al, bh))
+    rows = ah.shape[0]
+    both = d(jnp.concatenate([ah, al], axis=0), bh)
+    return both[:rows] + (d(ah, bl) + both[rows:])
 
 
 def diag_inverse(full):
@@ -280,7 +282,7 @@
     def take(k):
         settle(inbox.at[k], recv_sem.at[k])
         x_ref[:, pl.ds(pl.multiple_of(k * BLK, BLK), BLK)] = (
-            inbox[k].astype(jnp.float32).reshape(devices * slots, BLK).astype(jnp.bfloat16)
+            inbox[k].reshape(devices * slots, BLK)
         )
 
     def step(k, carry):
@@ -338,11 +340,17 @@
     s, t = whole_block(x_ref, wh, wl, n // BLK - 1, scale_ref[0, 0:1, :], scale_ref[1, 0:1, :])
     own = diag_inverse(s)
     last[:, done:] = own
-    last[:, :done] = -dot3(split(own), split(t), NN)
-    late = pltpu.make_async_copy(last, out_ref.at[pl.ds(done, BLK)], sems.at[1])
-    late.start()
-    early.wait()
-    late.wait()
+    t = split(t)
+    moves = [early]
+    for q, b0 in enumerate(range(0, BLK, PAN)):
+        e = b0 + PAN
+        part = split(own[b0:e, :e])
+        last[b0:e, :done] = -dot3(part, (t[0][:e], t[1][:e]), NN)
+        move = pltpu.make_async_copy(last.at[pl.ds(b0, PAN)], out_ref.at[pl.ds(done + b0, PAN)], sems.at[1 + q])
+        move.start()
+        moves.append(move)
+    for move in moves:
+        move.wait()
 
 
 def shards(captured, expert_ids):
@@ -390,7 +398,7 @@
         out_shape=jax.ShapeDtypeStruct((n, n), f32),
         in_specs=[vmem] * 5,
         out_specs=pl.BlockSpec(memory_space=pl.ANY),
-        scratch_shapes=[pltpu.VMEM((BLK, n), f32), pltpu.SemaphoreType.DMA((2,))],
+        scratch_shapes=[pltpu.VMEM((BLK, n), f32), pltpu.SemaphoreType.DMA((1 + BLK // PAN,))],
         compiler_params=pltpu.CompilerParams(vmem_limit_bytes=36 << 20),
         name="whiten_last",
     )(*parts)

time: 60.6 us -> 59.8 us (0.987)
  no operation moved by 1% of the time
where the time goes in v4:
time: 59.8 us; the launch traced here: 59.1 us
  Pallas kernels  58.9 us (98%)
    pallas_call x1, Pallas kernels, shards(): pl.pallas_call(exchange_kernel, out_shape=[pltpu.VMEM((done, n), f32), pl...  54.2 us
    pallas_call x1, Pallas kernels, shards(): pl.pallas_call(last_kernel, out_shape=jax.ShapeDtypeStruct((n, n), f32),...  4.73 us

profile of v4, /device:TPU:1, one launch (start us, length us, event | category | flops | bytes accessed | tf_op | source)
XLA Modules:
  0.0 59.1 jit_solution(6092041477865915884)
XLA Ops:
  0.0 54.2 %exchange_whiten.1 = (f32[896,1024]{1,0:T(8,128)S(1)}, bf16[896,896]{1,0:T(8,128)(2,1)S(1)}, bf16[896,896]{1,0:T(8,128)(2,1)S(1)}, bf16[1024,1024]{1,0:T(8,128)(2,1)S(1)}, f32[2,8,128]{2,1,0:T(8,128)S(1)}) custom-call(s32[8,64]{1,0:T(8,128)} %bitcast.2, bf16[64,8,1024]{2,1,0:T(8,128)(2,1)} %in_hbm.1), custom_call_target="tpu_custom_call" | custom-call | tf_op jit(solution)/shard_map/exchange_whiten/pallas_call | solution.py:368
  54.2 4.7 %whiten_last.1 = f32[1024,1024]{1,0:T(8,128)} custom-call(f32[896,1024]{1,0:T(8,128)S(1)} %get-tuple-element.10.o_ref, bf16[896,896]{1,0:T(8,128)(2,1)S(1)} %get-tuple-element.11.wh, bf16[896,896]{1,0:T(8,128)(2,1)S(1)} %get-tuple-element.12.wl, bf16[1024,1024]{1,0:T(8,128)(2,1)S(1)} %get-tuple-element.13.x_ref, f32[2,8,128]{2,1,0:T(8,128)S(1)} %get-tuple-element.14.scale_ref), custom_call_target="tpu_custom_call" | custom-call | tf_op jit(solution)/shard_map/whiten_last/pallas_call | solution.py:396

commit v5 on v4

--- a/solution.py
+++ b/solution.py
@@ -236,9 +236,9 @@
         return carry
 
     build(0)
-    build(1)
     pl.semaphore_wait(barrier, devices - 1)
     send(0)
+    build(1)
     counts = jnp.sum(onehot_f, axis=1, keepdims=True)
     squares = jnp.zeros((devices, BLK), jnp.float32)
     for c in range(steps):

time: 59.8 us -> 59.8 us (level)
  no operation moved by 1% of the time
where the time goes in v5:
time: 59.8 us; the launch traced here: 59.1 us
  Pallas kernels  58.9 us (98%)
    pallas_call x1, Pallas kernels, shards(): pl.pallas_call(exchange_kernel, out_shape=[pltpu.VMEM((done, n), f32), pl...  54.2 us
    pallas_call x1, Pallas kernels, shards(): pl.pallas_call(last_kernel, out_shape=jax.ShapeDtypeStruct((n, n), f32),...  4.73 us

profile of v5, /device:TPU:1, one launch (start us, length us, event | category | flops | bytes accessed | tf_op | source)
XLA Modules:
  0.0 59.1 jit_solution(8180867311424894015)
XLA Ops:
  0.0 54.2 %exchange_whiten.1 = (f32[896,1024]{1,0:T(8,128)S(1)}, bf16[896,896]{1,0:T(8,128)(2,1)S(1)}, bf16[896,896]{1,0:T(8,128)(2,1)S(1)}, bf16[1024,1024]{1,0:T(8,128)(2,1)S(1)}, f32[2,8,128]{2,1,0:T(8,128)S(1)}) custom-call(s32[8,64]{1,0:T(8,128)} %bitcast.2, bf16[64,8,1024]{2,1,0:T(8,128)(2,1)} %in_hbm.1), custom_call_target="tpu_custom_call" | custom-call | tf_op jit(solution)/shard_map/exchange_whiten/pallas_call | solution.py:368
  54.2 4.7 %whiten_last.1 = f32[1024,1024]{1,0:T(8,128)} custom-call(f32[896,1024]{1,0:T(8,128)S(1)} %get-tuple-element.10.o_ref, bf16[896,896]{1,0:T(8,128)(2,1)S(1)} %get-tuple-element.11.wh, bf16[896,896]{1,0:T(8,128)(2,1)S(1)} %get-tuple-element.12.wl, bf16[1024,1024]{1,0:T(8,128)(2,1)S(1)} %get-tuple-element.13.x_ref, f32[2,8,128]{2,1,0:T(8,128)S(1)} %get-tuple-element.14.scale_ref), custom_call_target="tpu_custom_call" | custom-call | tf_op jit(solution)/shard_map/whiten_last/pallas_call | solution.py:396

commit v6 on v5

--- a/solution.py
+++ b/solution.py
@@ -160,8 +160,10 @@
         pl.semaphore_signal(barrier, inc=1, device_id=place(offset)[1], device_id_type=pl.DeviceIdType.MESH)
         return carry
 
-    load = pltpu.make_async_copy(in_hbm, in_ref, in_sem)
-    load.start()
+    loads = []
+    for i, at in enumerate((pl.ds(0, BLK), pl.ds(BLK, n - BLK))):
+        loads.append(pltpu.make_async_copy(in_hbm.at[:, :, at], in_ref.at[:, :, at], in_sem.at[i]))
+        loads[i].start()
     def far_first(step, carry):
         exp, tok = lax.axis_index("exp"), lax.axis_index("tok")
         toks = devices // exp_size
@@ -199,7 +201,7 @@
     for i in range(0, devices * slots, BLK):
         row = lax.broadcasted_iota(jnp.int32, (BLK, entries), 0) + i
         pick[i : i + BLK, :] = (row == target).astype(jnp.float32).astype(jnp.bfloat16)
-    load.wait()
+    loads[0].wait()
 
     def build(c):
         part = lax.dot_general(
@@ -238,6 +240,7 @@
     build(0)
     pl.semaphore_wait(barrier, devices - 1)
     send(0)
+    loads[1].wait()
     build(1)
     counts = jnp.sum(onehot_f, axis=1, keepdims=True)
     squares = jnp.zeros((devices, BLK), jnp.float32)
@@ -385,7 +388,7 @@
             box,
             stat,
             stat,
-            pltpu.SemaphoreType.DMA,
+            pltpu.SemaphoreType.DMA((2,)),
             pltpu.SemaphoreType.DMA((steps,)),
             pltpu.SemaphoreType.DMA((steps,)),
             pltpu.SemaphoreType.DMA((2,)),

time: 59.8 us -> 60 us (level)
  no operation moved by 1% of the time
where the time goes in v6:
time: 60 us; the launch traced here: 59.1 us
  Pallas kernels  58.9 us (98%)
    pallas_call x1, Pallas kernels, shards(): pl.pallas_call(exchange_kernel, out_shape=[pltpu.VMEM((done, n), f32), pl...  54.2 us
    pallas_call x1, Pallas kernels, shards(): pl.pallas_call(last_kernel, out_shape=jax.ShapeDtypeStruct((n, n), f32),...  4.72 us

profile of v6, /device:TPU:1, one launch (start us, length us, event | category | flops | bytes accessed | tf_op | source)
XLA Modules:
  0.0 59.1 jit_solution(16679975776292795021)
XLA Ops:
  0.0 54.2 %exchange_whiten.1 = (f32[896,1024]{1,0:T(8,128)S(1)}, bf16[896,896]{1,0:T(8,128)(2,1)S(1)}, bf16[896,896]{1,0:T(8,128)(2,1)S(1)}, bf16[1024,1024]{1,0:T(8,128)(2,1)S(1)}, f32[2,8,128]{2,1,0:T(8,128)S(1)}) custom-call(s32[8,64]{1,0:T(8,128)} %bitcast.2, bf16[64,8,1024]{2,1,0:T(8,128)(2,1)} %in_hbm.1), custom_call_target="tpu_custom_call" | custom-call | tf_op jit(solution)/shard_map/exchange_whiten/pallas_call | solution.py:371
  54.2 4.7 %whiten_last.1 = f32[1024,1024]{1,0:T(8,128)} custom-call(f32[896,1024]{1,0:T(8,128)S(1)} %get-tuple-element.10.o_ref, bf16[896,896]{1,0:T(8,128)(2,1)S(1)} %get-tuple-element.11.wh, bf16[896,896]{1,0:T(8,128)(2,1)S(1)} %get-tuple-element.12.wl, bf16[1024,1024]{1,0:T(8,128)(2,1)S(1)} %get-tuple-element.13.x_ref, f32[2,8,128]{2,1,0:T(8,128)S(1)} %get-tuple-element.14.scale_ref), custom_call_target="tpu_custom_call" | custom-call | tf_op jit(solution)/shard_map/whiten_last/pallas_call | solution.py:399
